TPU v7x, 256 devices: a whole 4x4x8 slice. The times are simulated.
256 devices in a mesh: blk: 32 (over y_hi, z, core), rep: 8 (over x, y_lo).
Axes of the slice: x: 4, y: 4 (y_hi: 2, y_lo: 2; y = y_hi * 2 + y_lo), z: 8, core: 2. Of those that a mesh axis runs over, the one named last changes fastest.
Arguments:
- features: float32 [32768, 128], P('blk'), may hold values from -6 to 6
- factors: float32 [32768, 128], P('blk'), may hold values from -2.4 to 2.4
Outputs:
- grads: float32 [32768, 128], P(('blk', 'rep'))
All inputs are finite; a program needn't handle non-finite values.
Results may differ from a plain program's by a relative error of at most 0.00018.
Values sent between devices are 32-bit elements; how exact they have to be, the bound alone decides.
A program may use at most 128 MiB of HBM per device.

v0:
```python
import jax
import jax.numpy as jnp
from jax import lax
from jax.sharding import PartitionSpec as P


def pair_terms(own_feat, own_fac, part_feat, part_fac):
    hi = lax.Precision.HIGHEST
    width = own_feat.shape[1]
    rank = own_fac.shape[1] // 2
    cross = jnp.dot(own_feat, part_feat.T, precision=hi)
    own_sq = jnp.sum(own_feat * own_feat, axis=1)
    part_sq = jnp.sum(part_feat * part_feat, axis=1)
    kernel = jnp.exp(-(own_sq[:, None] + part_sq[None, :] - 2.0 * cross) / (2.0 * width))
    coupling = jnp.dot(own_fac[:, :rank], part_fac[:, rank:].T, precision=hi)
    coupling = coupling + jnp.dot(own_fac[:, rank:], part_fac[:, :rank].T, precision=hi)
    weight = coupling * kernel
    own_term = jnp.sum(weight, axis=1)[:, None] * own_feat - jnp.dot(
        weight, part_feat, precision=hi
    )
    return (weight, -own_term / width)


def body(features, factors):
    count = features.shape[0]
    replicas = lax.axis_size("rep")
    share = count // replicas
    first = lax.axis_index("rep") * share
    slice_feat = lax.dynamic_slice_in_dim(features, first, share, 0)
    slice_fac = lax.dynamic_slice_in_dim(factors, first, share, 0)
    weight, own_term = pair_terms(
        features,
        factors,
        lax.all_gather(slice_feat, "blk", axis=0, tiled=True),
        lax.all_gather(slice_fac, "blk", axis=0, tiled=True),
    )
    summed = lax.psum_scatter(own_term, "rep", scatter_dimension=0, tiled=True)
    return summed


def solution(mesh):
    placed = (P("blk", None), P("blk", None))
    return jax.shard_map(
        body, mesh=mesh, in_specs=placed, out_specs=P(("blk", "rep"), None), check_vma=False
    )
```

profile of v0, /device:TPU:32, one launch (start us, length us, event | category | flops | bytes accessed | tf_op | source)
XLA Modules:
  0.0 273.3 jit_solution(17942812913476998213)
XLA Ops:
  6.5 0.0 copy-start.3
  6.5 0.0 all-gather.3.cloned.1.call-start
  6.5 1.5 constant_dynamic-slice_fusion.1
  8.1 0.0 all-gather.3.cloned.1.call-update
  8.1 0.0 all-gather.5.cloned.1.call-start
  8.2 1.5 constant_dynamic-slice_fusion
  9.6 0.0 all-gather.5.cloned.1.call-update
  9.7 0.0 reduce-scatter.2.cloned.1.call-start
  9.7 1.2 multiply_reduce_fusion.1
  11.0 0.0 copy-start.2
  11.0 80.9 %all-gather.3.cloned.1.call-done = f32[4096,128]{1,0:T(8,128)} async-done(((f32[128,128]{1,0:T(8,128)}), f32[4096,128]{1,0:T(8,128)}) %all-gather.3.cloned.1.call-update) | async-done | bytes 2097168 | tf_op jit(solution)/shard_map/all_gather | solution.py:35
  91.8 0.0 copy-start.1
  91.8 17.7 %fusion.4 = f32[4096,1024]{1,0:T(8,128)} fusion(f32[4096,128]{1,0:T(8,128)} %all-gather.3.cloned.1.call-done, f32[1024,128]{1,0:T(8,128)} %param.3), kind=kOutput, calls=%fused_computation.5 | convolution fusion | flops 3221225472 | bytes 19398656 | tf_op jit(solution)/shard_map/dot_general | solution.py:16
  109.5 0.0 copy-done.3
  109.5 0.0 copy-done.1
  109.5 16.1 %fusion.6 = f32[4096,1024]{1,0:T(8,128)} fusion(f32[4096,128]{1,0:T(8,128)S(1)} %copy-done.1, f32[1024,128]{1,0:T(8,128)S(1)} %copy-done.3), kind=kOutput, calls=%fused_computation.7 | convolution fusion | flops 3221225472 | bytes 19398656 | tf_op jit(solution)/shard_map/dot_general | solution.py:15
  125.6 45.3 %all-gather.5.cloned.1.call-done = f32[4096,128]{1,0:T(8,128)} async-done(((f32[128,128]{1,0:T(8,128)}), f32[4096,128]{1,0:T(8,128)}) %all-gather.5.cloned.1.call-update) | async-done | bytes 2097168 | tf_op jit(solution)/shard_map/all_gather | solution.py:34
  171.0 2.2 multiply_reduce_fusion
  173.2 0.0 copy-done.2
  173.2 0.0 copy-start
  173.2 25.9 %fusion.12 = (f32[1024]{0:T(1024)S(1)}, f32[1024,4096]{0,1:T(8,128)}) fusion(f32[4096,128]{1,0:T(8,128)} %all-gather.5.cloned.1.call-done, f32[1024,128]{1,0:T(8,128)S(1)} %copy-done.2, f32[4096]{0:T(1024)S(1)} %multiply_reduce_fusion, f32[1024]{0:T(1024)S(1)} %multiply_reduce_fusion.1, f32[4096,1024]{1,0:T(8,128)} %fusion.6, f32[4096,1024]{1,0:T(8,128)} %fusion.4), kind=kOutput, calls=%fused_computation.18 | convolution fusion | flops 6476004352 | bytes 52977664 | tf_op jit(solution)/shard_map/dot_general | solution.py:11
  199.1 0.0 copy-done
  199.1 29.5 %fusion.9 = f32[1024,128]{1,0:T(8,128)} fusion(f32[1024,4096]{0,1:T(8,128)} %get-tuple-element.6, f32[4096,128]{1,0:T(8,128)S(1)} %copy-done, f32[1024,128]{1,0:T(8,128)S(1)} %copy-done.2, f32[1024]{0:T(1024)S(1)} %get-tuple-element.5), kind=kOutput, calls=%fused_computation.12 | convolution fusion | flops 6442975232 | bytes 19927040 | tf_op jit(solution)/shard_map/dot_general | solution.py:18
  228.6 0.0 reduce-scatter.2.cloned.1.call-update
  228.6 38.1 %reduce-scatter.2.cloned.1.call-done = f32[128,128]{1,0:T(8,128)} async-done(((f32[1024,128]{1,0:T(8,128)}), f32[128,128]{1,0:T(8,128)}) %reduce-scatter.2.cloned.1.call-update) | async-done | bytes 65552 | tf_op jit(solution)/shard_map/reduce_scatter | solution.py:37
Async XLA Ops:
  6.5 103.0 %copy-start.3 = (f32[1024,128]{1,0:T(8,128)S(1)}, f32[1024,128]{1,0:T(8,128)}, u32[]{:S(2)}) copy-start(f32[1024,128]{1,0:T(8,128)} %param.3) | copy-start | bytes 1572868
  6.5 85.3 %all-gather.3.cloned.1.call-start = ((), (), s32[]{:S(2)}) async-start(), calls=%async_computation.1 | async-start | bytes 2162688 | tf_op jit(solution)/shard_map/all_gather | solution.py:35
  8.1 162.9 %all-gather.5.cloned.1.call-start = ((), (), s32[]{:S(2)}) async-start(), calls=%async_computation.2 | async-start | bytes 2162688 | tf_op jit(solution)/shard_map/all_gather | solution.py:34
  9.7 257.1 %reduce-scatter.2.cloned.1.call-start = ((), (), s32[]{:S(2)}) async-start(), calls=%async_computation.3 | async-start | bytes 589824 | tf_op jit(solution)/shard_map/reduce_scatter | solution.py:37
  11.0 162.2 %copy-start.2 = (f32[1024,128]{1,0:T(8,128)S(1)}, f32[1024,128]{1,0:T(8,128)}, u32[]{:S(2)}) copy-start(f32[1024,128]{1,0:T(8,128)} %param.2) | copy-start | bytes 1572868
  91.8 17.7 %copy-start.1 = (f32[4096,128]{1,0:T(8,128)S(1)}, f32[4096,128]{1,0:T(8,128)}, u32[]{:S(2)}) copy-start(f32[4096,128]{1,0:T(8,128)} %all-gather.3.cloned.1.call-done) | copy-start | bytes 6291460
  173.2 25.9 %copy-start = (f32[4096,128]{1,0:T(8,128)S(1)}, f32[4096,128]{1,0:T(8,128)}, u32[]{:S(2)}) copy-start(f32[4096,128]{1,0:T(8,128)} %all-gather.5.cloned.1.call-done) | copy-start | bytes 6291460
Sparse Core Ops, SparseCore 0:
  10.1 81.6 all-gather.2
  94.6 76.3 all-gather.4
  228.7 37.9 reduce-scatter.1
where the time goes:
time: 273 us
  waiting for transfers between devices  164 us (60%)
  matrix products  89.2 us (33%)
  between operations  13.2 us (5%)
  other arithmetic  3.45 us (1%)
  local copies, waits for them, and re-layouts  3.04 us (1%)
    all_gather x1, waiting for transfers between devices, body(): lax.all_gather(slice_fac, 'blk', axis=0, tiled=True)  80.9 us
    all_gather x1, waiting for transfers between devices, body(): lax.all_gather(slice_feat, 'blk', axis=0, tiled=True)  45.3 us
    reduce_scatter x1, waiting for transfers between devices, body(): summed = lax.psum_scatter(own_term, 'rep', scatter_dimension=0, tiled=True)  38.1 us
    dot_general x1, matrix products, pair_terms(): jnp.dot(weight, part_feat, precision=hi)  29.5 us
    dot_general x1, matrix products, pair_terms(): cross = jnp.dot(own_feat, part_feat.T, precision=hi)  25.9 us
    dot_general x1, matrix products, pair_terms(): jnp.dot(own_fac[:, rank:], part_fac[:, :rank].T, precision=hi)  17.7 us
    dot_general x1, matrix products, pair_terms(): coupling = jnp.dot(own_fac[:, :rank], part_fac[:, rank:].T, precision=hi)  16.1 us
  transfers between devices with their start and end apart: 3, of which 3 were waited for; matrix products, arithmetic and copies ran while one was open for 13% of the time, Pallas kernels for 0%

commit v1 on v0

--- a/solution.py
+++ b/solution.py
@@ -32,7 +32,9 @@
         features,
         factors,
         lax.all_gather(slice_feat, "blk", axis=0, tiled=True),
-        lax.all_gather(slice_fac, "blk", axis=0, tiled=True),
+        jnp.concatenate(
+            lax.all_to_all(jnp.stack([slice_fac] * lax.axis_size("blk")), "blk", 0, 0), axis=0
+        ),
     )
     summed = lax.psum_scatter(own_term, "rep", scatter_dimension=0, tiled=True)
     return summed

time: 273 us -> 213 us (0.78)
  waiting for transfers between devices: 164 us -> 91.3 us
  starting transfers between devices: 0.09 us -> 11.4 us
    all_gather x1 -> x0, waiting for transfers between devices: 80.9 us -> none  [body(): lax.all_gather(slice_fac, 'blk', axis=0, tiled=True)]
    all_to_all x0 -> x1, waiting for transfers between devices: none -> 52.5 us  [body(): lax.all_to_all(jnp.stack([slice_fac] * lax.axis_size('blk')), 'blk', 0, 0)]
    all_gather x1, waiting for transfers between devices: 45.3 us -> 0.6 us  [body(): lax.all_gather(slice_feat, 'blk', axis=0, tiled=True)]
    all_to_all x0 -> x1, starting transfers between devices: none -> 11.4 us  [body(): lax.all_to_all(jnp.stack([slice_fac] * lax.axis_size('blk')), 'blk', 0, 0)]
  transfers between devices with their start and end apart: 3 -> 3, of which waited for: 3 -> 3; matrix products, arithmetic and copies ran while one was open for 13% -> 17% of each run, Pallas kernels for 0% -> 0%
where the time goes in v1:
time: 213 us; the launch traced here: 212 us
  waiting for transfers between devices  91.3 us (43%)
  matrix products  88.8 us (42%)
  between operations  13.5 us (6%)
  starting transfers between devices  11.4 us (5%)
  local copies, waits for them, and re-layouts  3.99 us (2%)
  other arithmetic  3.45 us (2%)
    all_to_all x1, waiting for transfers between devices, body(): lax.all_to_all(jnp.stack([slice_fac] * lax.axis_size('blk')), 'blk', 0, 0)  52.5 us
    reduce_scatter x1, waiting for transfers between devices, body(): summed = lax.psum_scatter(own_term, 'rep', scatter_dimension=0, tiled=True)  38.2 us
    dot_general x1, matrix products, pair_terms(): jnp.dot(weight, part_feat, precision=hi)  29.5 us
    dot_general x1, matrix products, pair_terms(): cross = jnp.dot(own_feat, part_feat.T, precision=hi)  25.8 us
    dot_general x1, matrix products, pair_terms(): jnp.dot(own_fac[:, rank:], part_fac[:, :rank].T, precision=hi)  17.3 us
    dot_general x1, matrix products, pair_terms(): coupling = jnp.dot(own_fac[:, :rank], part_fac[:, rank:].T, precision=hi)  16.1 us
    all_to_all x1, starting transfers between devices, body(): lax.all_to_all(jnp.stack([slice_fac] * lax.axis_size('blk')), 'blk', 0, 0)  11.4 us
  transfers between devices with their start and end apart: 3, of which 3 were waited for; matrix products, arithmetic and copies ran while one was open for 17% of the time, Pallas kernels for 0%

profile of v1, /device:TPU:32, one launch (start us, length us, event | category | flops | bytes accessed | tf_op | source)
XLA Modules:
  0.0 212.4 jit_solution(6651676999008498699)
XLA Ops:
  6.5 0.0 copy-start.2
  6.5 0.9 constant_dynamic-slice_fusion.1
  7.5 1.6 stack.2
  9.0 11.4 %all-to-all-start = ((f32[32,128,128]{2,1,0:T(8,128)}), f32[32,128,128]{2,1,0:T(8,128)S(1)}, u32[]{:S(2)}, u32[]{:S(2)}) async-start(f32[32,128,128]{2,1,0:T(8,128)} %stack.2), calls=%async_computation | async-start | bytes 4194304 | tf_op jit(solution)/shard_map/all_to_all | solution.py:36
  20.4 0.0 all-gather.2.cloned.1.call-start
  20.4 1.5 constant_dynamic-slice_fusion
  21.9 0.0 all-gather.2.cloned.1.call-update
  22.0 0.0 reduce-scatter.2.cloned.1.call-start
  22.0 1.2 multiply_reduce_fusion.1
  23.3 52.5 %all-to-all-done = f32[32,128,128]{2,1,0:T(8,128)S(1)} async-done(((f32[32,128,128]{2,1,0:T(8,128)}), f32[32,128,128]{2,1,0:T(8,128)S(1)}, u32[]{:S(2)}, u32[]{:S(2)}) %all-to-all-start) | async-done | bytes 2097184 | tf_op jit(solution)/shard_map/all_to_all | solution.py:36
  75.8 0.0 copy-start.1
  75.8 17.3 %fusion.4 = f32[4096,1024]{1,0:T(8,128)} fusion(f32[4096,128]{1,0:T(8,128)S(1)} %bitcast.17, f32[1024,128]{1,0:T(8,128)} %param.3), kind=kOutput, calls=%fused_computation.5 | convolution fusion | flops 3221225472 | bytes 19398656 | tf_op jit(solution)/shard_map/dot_general | solution.py:16
  93.1 0.0 copy-done.2
  93.1 16.1 %fusion.6 = f32[4096,1024]{1,0:T(8,128)} fusion(f32[4096,128]{1,0:T(8,128)S(1)} %bitcast.18, f32[1024,128]{1,0:T(8,128)S(1)} %copy-done.2), kind=kOutput, calls=%fused_computation.7 | convolution fusion | flops 3221225472 | bytes 19398656 | tf_op jit(solution)/shard_map/dot_general | solution.py:15
  109.2 0.6 all-gather.2.cloned.1.call-done
  109.8 2.2 %multiply_reduce_fusion = f32[4096]{0:T(1024)S(1)} fusion(f32[4096,128]{1,0:T(8,128)} %all-gather.2.cloned.1.call-done), kind=kLoop, calls=%fused_computation.9 | loop fusion | flops 1044480 | bytes 2113536 | tf_op jit(solution)/shard_map/reduce_sum | solution.py:13
  112.0 0.0 copy-done.1
  112.0 0.0 copy-start
  112.1 25.8 %fusion.12 = (f32[1024]{0:T(1024)S(1)}, f32[1024,4096]{0,1:T(8,128)}) fusion(f32[4096,128]{1,0:T(8,128)} %all-gather.2.cloned.1.call-done, f32[1024,128]{1,0:T(8,128)S(1)} %copy-done.1, f32[4096]{0:T(1024)S(1)} %multiply_reduce_fusion, f32[1024]{0:T(1024)S(1)} %multiply_reduce_fusion.1, f32[4096,1024]{1,0:T(8,128)} %fusion.6, f32[4096,1024]{1,0:T(8,128)} %fusion.4), kind=kOutput, calls=%fused_computation.18 | convolution fusion | flops 6476004352 | bytes 52977664 | tf_op jit(solution)/shard_map/dot_general | solution.py:11
  137.9 0.0 copy-done
  137.9 29.5 %fusion.9 = f32[1024,128]{1,0:T(8,128)} fusion(f32[1024,4096]{0,1:T(8,128)} %get-tuple-element.6, f32[4096,128]{1,0:T(8,128)S(1)} %copy-done, f32[1024,128]{1,0:T(8,128)S(1)} %copy-done.1, f32[1024]{0:T(1024)S(1)} %get-tuple-element.5), kind=kOutput, calls=%fused_computation.12 | convolution fusion | flops 6442975232 | bytes 19927040 | tf_op jit(solution)/shard_map/dot_general | solution.py:18
  167.4 0.0 reduce-scatter.2.cloned.1.call-update
  167.4 38.2 %reduce-scatter.2.cloned.1.call-done = f32[128,128]{1,0:T(8,128)} async-done(((f32[1024,128]{1,0:T(8,128)}), f32[128,128]{1,0:T(8,128)}) %reduce-scatter.2.cloned.1.call-update) | async-done | bytes 65552 | tf_op jit(solution)/shard_map/reduce_scatter | solution.py:39
Async XLA Ops:
  6.5 86.6 %copy-start.2 = (f32[1024,128]{1,0:T(8,128)S(1)}, f32[1024,128]{1,0:T(8,128)}, u32[]{:S(2)}) copy-start(f32[1024,128]{1,0:T(8,128)} %param.3) | copy-start | bytes 1572868
  9.0 66.8 %all-to-all-start = ((f32[32,128,128]{2,1,0:T(8,128)}), f32[32,128,128]{2,1,0:T(8,128)S(1)}, u32[]{:S(2)}, u32[]{:S(2)}) async-start(f32[32,128,128]{2,1,0:T(8,128)} %stack.2), calls=%async_computation | async-start | bytes 4194304 | tf_op jit(solution)/shard_map/all_to_all | solution.py:36
  20.4 89.4 %all-gather.2.cloned.1.call-start = ((), (), s32[]{:S(2)}) async-start(), calls=%async_computation.2 | async-start | bytes 2162688 | tf_op jit(solution)/shard_map/all_gather | solution.py:34
  22.0 183.6 %reduce-scatter.2.cloned.1.call-start = ((), (), s32[]{:S(2)}) async-start(), calls=%async_computation.3 | async-start | bytes 589824 | tf_op jit(solution)/shard_map/reduce_scatter | solution.py:39
  75.8 36.2 %copy-start.1 = (f32[1024,128]{1,0:T(8,128)S(1)}, f32[1024,128]{1,0:T(8,128)}, u32[]{:S(2)}) copy-start(f32[1024,128]{1,0:T(8,128)} %param.2) | copy-start | bytes 1572868
  112.0 25.8 %copy-start = (f32[4096,128]{1,0:T(8,128)S(1)}, f32[4096,128]{1,0:T(8,128)}, u32[]{:S(2)}) copy-start(f32[4096,128]{1,0:T(8,128)} %all-gather.2.cloned.1.call-done) | copy-start | bytes 6291460
Sparse Core Ops, SparseCore 0:
  24.0 85.7 all-gather.1
  167.5 38.0 reduce-scatter.1
